TPU v7x, 256 devices: a whole 4x4x8 slice. The times are simulated.
256 devices in a mesh: pair: 32 (over y, z), aux: 8 (over x, core).
Axes of the slice: x: 4, y: 4, z: 8, core: 2. Of those that a mesh axis runs over, the one named last changes fastest.
Arguments:
- three_center: bfloat16 [8192, 32, 2048], P(('pair', 'aux')), may hold values from -1 to 1
- panel: bfloat16 [512, 64], P('pair'), may hold values from -6 to 6
- metric: float32 [256, 64, 64], P(('pair', 'aux')), may hold values from -0.5 to 1.6
- screen: int32 [32, 256, 1], P(None, 'aux'), may hold values from 0 to 31; in each aligned block of 32 rows (0 to 31, 32 to 63, ..., all dimensions but the last counted through in order) at most 2 rows name the same one
- pair_blocks: int32 [32, 256, 2], P(None, 'aux'), may hold values from 0 to 15
Outputs:
- fitted: bfloat16 [256, 512, 4096], P(('pair', 'aux'))
- exchange: float32 [512, 512], P(('pair', 'aux'))
Inputs may be any that keep to these rules, and one draw needn't show every extreme that they name: `screen`: in the list of one device no pair index is named by more than 2 slots, and in some lists one is named exactly 2 times.
All inputs are finite; a program needn't handle non-finite values.
Results may differ from a plain program's by a relative error of at most 0.0049.
Values may be sent and summed in bfloat16 or wider, within the bound.
No kernel may reach another device: no remote copies, remote signals or barrier semaphores. Data moves between devices by JAX's collectives and lax.ppermute only.
A program may use at most 192 MiB of HBM per device.

v0:
```python
import jax
import jax.numpy as jnp
from jax import lax
from jax.sharding import PartitionSpec as P


def shards(three_center, panel, metric, screen, pair_blocks):
    pair_count = lax.axis_size("pair")
    column_count = lax.axis_size("aux")
    own_index = lax.axis_index("pair")
    slot_count = three_center.shape[0]
    basis_width = three_center.shape[1]
    aux_width = metric.shape[1]
    orbital_count = panel.shape[1]
    capacity = max(2, 2 * slot_count // pair_count)
    buffer_rows = pair_count * capacity
    whole_panel = lax.all_gather(panel, "pair", axis=0, tiled=True)
    basis_total = whole_panel.shape[0]
    block_count = basis_total // basis_width
    panel_blocks = whole_panel.reshape(block_count, basis_width * orbital_count)
    targets = screen[:, :, 0]
    mu_blocks = pair_blocks[:, :, 0]
    nu_blocks = pair_blocks[:, :, 1]
    slot_ids = jnp.arange(slot_count)
    earlier = slot_ids[None, :] < slot_ids[:, None]
    same_target = targets[:, :, None] == targets[:, None, :]
    ranks = jnp.sum(same_target & earlier[None, :, :], axis=2)
    own_targets = lax.dynamic_index_in_dim(targets, own_index, 0, keepdims=False)
    own_ranks = lax.dynamic_index_in_dim(ranks, own_index, 0, keepdims=False)
    own_nu = lax.dynamic_index_in_dim(nu_blocks, own_index, 0, keepdims=False)
    position = own_targets * capacity + own_ranks
    packing = (jnp.arange(buffer_rows)[:, None] == position[None, :]).astype(jnp.bfloat16)
    hits = (targets == own_index)[:, None, :] & (
        ranks[:, None, :] == jnp.arange(capacity)[None, :, None]
    )
    valid = jnp.any(hits, axis=2).reshape(buffer_rows)
    recv_mu = jnp.sum(jnp.where(hits, mu_blocks[:, None, :], 0), axis=2).reshape(buffer_rows)
    block_size = basis_width * aux_width * orbital_count
    own_pick = (own_nu[:, None] == jnp.arange(block_count)[None, :]).astype(jnp.bfloat16)
    own_panel = jnp.dot(own_pick, panel_blocks, preferred_element_type=jnp.float32).astype(
        jnp.bfloat16
    )
    own_panel = own_panel.reshape(slot_count, basis_width, orbital_count)
    blocks_local = three_center.reshape(slot_count, basis_width, aux_width, basis_width)
    transformed = jnp.einsum(
        "smqn,sni->smqi", blocks_local, own_panel, preferred_element_type=jnp.float32
    )
    transformed = transformed.astype(jnp.bfloat16).reshape(slot_count, block_size)
    outgoing = jnp.dot(packing, transformed, preferred_element_type=jnp.float32).astype(
        jnp.bfloat16
    )
    outgoing = outgoing.reshape(pair_count, capacity, block_size)
    arrived = lax.all_to_all(outgoing, "pair", split_axis=0, concat_axis=0, tiled=True)
    received = arrived.reshape(buffer_rows, block_size)
    placing = ((recv_mu[None, :] == jnp.arange(block_count)[:, None]) & valid[None, :]).astype(
        jnp.bfloat16
    )
    coefficients = jnp.dot(placing, received, preferred_element_type=jnp.float32)
    coefficients = coefficients.reshape(basis_total, aux_width, orbital_count)
    fitted = jnp.einsum("pq,rqi->rpi", metric[0], coefficients, precision=lax.Precision.HIGHEST)
    fitted = fitted.astype(jnp.bfloat16).reshape(basis_total, aux_width * orbital_count)
    summed_rows = lax.psum_scatter(
        lax.dot_general(
            fitted, fitted, (((1,), (1,)), ((), ())), preferred_element_type=jnp.float32
        ),
        ("pair", "aux"),
        scatter_dimension=0,
        tiled=True,
    )
    norm_factor = 1.0 / (pair_count * column_count * aux_width * orbital_count)
    return (fitted[None], summed_rows * norm_factor)


def solution(mesh):
    return jax.shard_map(
        shards,
        mesh=mesh,
        in_specs=(
            P(("pair", "aux"), None, None),
            P("pair", None),
            P(("pair", "aux"), None, None),
            P(None, "aux", None),
            P(None, "aux", None),
        ),
        out_specs=(P(("pair", "aux"), None, None), P(("pair", "aux"), None)),
        check_vma=False,
    )
```

profile of v0, /device:TPU:32, one launch (start us, length us, event | category | flops | bytes accessed | tf_op | source)
XLA Modules:
  0.0 882.4 jit_solution(821267720324397668)
XLA Ops:
  7.2 0.0 copy-start
  7.2 0.9 fusion.16
  8.1 1.6 convert_reduce_fusion
  9.6 0.7 fusion.15
  10.3 45.7 %all_gather.3 = bf16[512,64]{1,0:T(8,128)(2,1)S(1)} all-gather(bf16[16,64]{1,0:T(8,128)(2,1)} %param.6), channel_id=1, replica_groups=mesh['pair'=32,'aux'=8] {'pair'}, dimensions={0}, use_global_device_ids=true | all-gather | bytes 67584 | tf_op jit(solution)/shard_map/all_gather | solution.py:17
  56.1 0.2 reshape.66
  56.2 0.2 convolution_convert_fusion.1
  56.5 0.2 reshape.73
  56.7 19.5 %reshape.68 = bf16[32,32,64,32]{3,2,1,0:T(8,128)(2,1)} reshape(bf16[32,32,2048]{2,1,0:T(8,128)(2,1)} %param.5) | data formatting | bytes 8388608 | tf_op jit(solution)/shard_map/reshape | solution.py:44
  76.2 21.9 %convert_bitcast_fusion = bf16[32,32,64,64]{2,3,1,0:T(8,128)(2,1)} fusion(bf16[32,32,64,32]{3,2,1,0:T(8,128)(2,1)} %reshape.68, bf16[32,32,64,1]{2,1,0,3:T(8,128)(2,1)S(1)} %reshape.73), kind=kOutput, calls=%fused_computation.1 | convolution fusion | flops 272629760 | bytes 12713984 | tf_op jit(solution)/shard_map/smqn,sni->smqi/dot_general | solution.py:45
  98.1 22.5 %copy.26 = bf16[32,32,64,64]{3,2,1,0:T(8,128)(2,1)} copy(bf16[32,32,64,64]{2,3,1,0:T(8,128)(2,1)} %convert_bitcast_fusion) | data formatting | bytes 16777216 | tf_op jit(solution)/shard_map/convert_element_type | solution.py:48
  120.7 15.9 %reshape.69 = bf16[32,131072]{1,0:T(8,128)(2,1)} reshape(bf16[32,32,64,64]{3,2,1,0:T(8,128)(2,1)} %copy.26) | data formatting | bytes 16777216 | tf_op jit(solution)/shard_map/reshape | solution.py:48
  136.6 11.4 %convolution_convert_fusion = bf16[64,131072]{1,0:T(8,128)(2,1)} fusion(bf16[32,131072]{1,0:T(8,128)(2,1)} %reshape.69, s32[32]{0:T(128)S(1)} %fusion.15), kind=kOutput, calls=%fused_computation | convolution fusion | flops 545261568 | bytes 25165952 | tf_op jit(solution)/shard_map/dot_general | solution.py:49
  148.0 17.0 %reshape.70 = bf16[32,2,131072]{2,1,0:T(2,128)(2,1)} reshape(bf16[64,131072]{1,0:T(8,128)(2,1)} %convolution_convert_fusion) | data formatting | bytes 33554432 | tf_op jit(solution)/shard_map/reshape | solution.py:52
  165.0 0.0 copy-start.2
  165.0 7.1 all-to-all-start
  172.1 0.0 all-reduce.3.cloned.1.call-start
  172.2 0.0 copy-done.2
  172.2 0.1 fusion.3
  172.3 0.1 copy.24
  172.4 0.1 and.31
  172.5 0.1 select_reduce_fusion
  172.7 0.1 copy.23
  172.7 0.1 eq.89
  172.9 354.2 %all-to-all-done = bf16[32,2,131072]{2,1,0:T(2,128)(2,1)} async-done(((bf16[32,2,131072]{2,1,0:T(2,128)(2,1)}), bf16[32,2,131072]{2,1,0:T(2,128)(2,1)}, u32[]{:S(2)}, u32[]{:S(2)}) %all-to-all-start) | async-done | bytes 16777248 | tf_op jit(solution)/shard_map/all_to_all | solution.py:53
  527.0 16.2 %reshape.71 = bf16[64,131072]{1,0:T(8,128)(2,1)} reshape(bf16[32,2,131072]{2,1,0:T(2,128)(2,1)} %all-to-all-done) | data formatting | bytes 33554432 | tf_op jit(solution)/shard_map/reshape | solution.py:54
  543.3 11.3 %fusion.7 = f32[16,131072]{1,0:T(8,128)} fusion(bf16[64,131072]{1,0:T(8,128)(2,1)} %reshape.71, s32[64]{0:T(128)S(1)} %eq.89, pred[64]{0:T(512)(128)(4,1)S(1)} %and.31), kind=kOutput, calls=%fused_computation.20 | convolution fusion | flops 268437504 | bytes 25166144 | tf_op jit(solution)/shard_map/dot_general | solution.py:58
  554.5 17.4 %reshape.72 = f32[512,64,64]{2,1,0:T(8,128)} reshape(f32[16,131072]{1,0:T(8,128)} %fusion.7) | data formatting | bytes 16777216 | tf_op jit(solution)/shard_map/reshape | solution.py:59
  571.9 13.8 %copy.27 = f32[512,64,64]{0,1,2:T(8,128)} copy(f32[512,64,64]{2,1,0:T(8,128)} %reshape.72) | data formatting | bytes 16777216 | tf_op jit(solution)/shard_map/reshape | solution.py:59
  585.7 0.0 copy-done
  585.7 10.4 %convert_bitcast_fusion.1 = bf16[512,64,64]{0,1,2:T(8,128)(2,1)S(1)} fusion(f32[512,64,64]{0,1,2:T(8,128)} %copy.27, f32[1,64,64]{2,1,0:T(8,128)S(1)} %copy-done), kind=kOutput, calls=%fused_computation.2 | convolution fusion | flops 1612709888 | bytes 12599296 | tf_op jit(solution)/shard_map/pq,rqi->rpi/dot_general | solution.py:60
  596.1 0.0 copy-start.1
  596.2 2.0 copy-done.1
  598.2 3.4 convolution_bitcast_fusion
  601.5 0.0 all-reduce.3.cloned.1.call-update
  601.6 6.5 copy.28
  608.0 6.3 copy.29
  614.3 259.9 %all-reduce.3.cloned.1.call-done = f32[512,512]{1,0:T(8,128)} async-done(((f32[512,512]{1,0:T(8,128)}), f32[512,512]{1,0:T(8,128)}) %all-reduce.3.cloned.1.call-update) | async-done | bytes 1048592
  874.3 1.3 dynamic-slice_multiply_fusion
  (3 shorter events, 0.0 us)
Async XLA Ops:
  7.2 578.6 %copy-start = (f32[1,64,64]{2,1,0:T(8,128)S(1)}, f32[1,64,64]{2,1,0:T(8,128)}, u32[]{:S(2)}) copy-start(f32[1,64,64]{2,1,0:T(8,128)} %param.7) | copy-start | bytes 49156
  165.0 7.1 copy-start.2
  165.0 362.0 %all-to-all-start = ((bf16[32,2,131072]{2,1,0:T(2,128)(2,1)}), bf16[32,2,131072]{2,1,0:T(2,128)(2,1)}, u32[]{:S(2)}, u32[]{:S(2)}) async-start(bf16[32,2,131072]{2,1,0:T(2,128)(2,1)} %reshape.70), calls=%async_computation | async-start | bytes 33554432 | tf_op jit(solution)/shard_map/all_to_all | solution.py:53
  172.1 702.1 %all-reduce.3.cloned.1.call-start = ((), (), s32[]{:S(2)}) async-start(), calls=%async_computation.1 | async-start | bytes 2097152
  596.1 2.0 copy-start.1
Sparse Core Ops, SparseCore 0:
  601.7 272.5 all-reduce.2
where the time goes:
time: 887 us; the launch traced here: 882 us
  waiting for transfers between devices  614 us (69%)
  local copies, waits for them, and re-layouts  139 us (16%)
  matrix products  58.6 us (7%)
  blocking collectives  45.7 us (5%)
  between operations  14.1 us (2%)
    all_to_all x1, waiting for transfers between devices, shards(): lax.all_to_all(outgoing, 'pair', split_axis=0, concat_axis=0, tiled=True)  354 us
    unnamed x2, waiting for transfers between devices  260 us
    all_gather x1, blocking collectives, shards(): whole_panel = lax.all_gather(panel, 'pair', axis=0, tiled=True)  45.7 us
    reshape x2, local copies, waits for them, and re-layouts, shards(): coefficients = coefficients.reshape(basis_total, aux_width, orbital_count)  31.2 us
    convert_element_type x1, local copies, waits for them, and re-layouts, shards(): transformed.astype(jnp.bfloat16).reshape(slot_count, block_size)  22.5 us
    dot_general x1, matrix products, shards(): jnp.einsum('smqn,sni->smqi', blocks_local, own_panel, preferred_element_t...  21.9 us
    reshape x1, local copies, waits for them, and re-layouts, shards(): three_center.reshape(slot_count, basis_width, aux_width, basis_width)  19.5 us
  transfers between devices with their start and end apart: 2, of which 2 were waited for; matrix products, arithmetic and copies ran while one was open for 2% of the time, Pallas kernels for 0%

commit v1 on v0

v1 whole, which is shorter than its diff:
```python
import functools
import jax
import jax.numpy as jnp
from jax import lax
from jax.experimental import pallas as pl
from jax.experimental.pallas import tpu as pltpu
from jax.sharding import PartitionSpec as P

BF = jnp.bfloat16
F32 = jnp.float32


def iota(shape, dim):
    return lax.broadcasted_iota(jnp.int32, shape, dim)


def ones_where(mask):
    return jnp.where(mask, 1.0, 0.0).astype(BF)


def nt_dot(a, b):
    return lax.dot_general(a, b, (((1,), (1,)), ((), ())), preferred_element_type=F32)


def nn_dot(a, b):
    return jnp.dot(a, b, preferred_element_type=F32)


def pack_kernel(slots, position, blocks, out, held, in_sem, out_sem):
    def fetch(s):
        return pltpu.make_async_copy(blocks.at[s], held.at[s], in_sem.at[s])

    def put(s):
        return pltpu.make_async_copy(held.at[s], out.at[position[s]], out_sem.at[s])

    @pl.loop(0, slots)
    def _(s):
        fetch(s).start()

    @pl.loop(0, slots)
    def _(s):
        fetch(s).wait()
        put(s).start()

    @pl.loop(0, slots)
    def _(s):
        put(s).wait()


def pack(position, blocks, rows):
    slots, width, inner = blocks.shape
    return pl.pallas_call(
        functools.partial(pack_kernel, slots),
        out_shape=jax.ShapeDtypeStruct((rows, width, inner), blocks.dtype),
        grid_spec=pltpu.PrefetchScalarGridSpec(
            num_scalar_prefetch=1,
            grid=(1,),
            in_specs=[pl.BlockSpec(memory_space=pl.ANY)],
            out_specs=pl.BlockSpec(memory_space=pl.ANY),
            scratch_shapes=[
                pltpu.VMEM((slots, width, inner), blocks.dtype),
                pltpu.SemaphoreType.DMA((slots,)),
                pltpu.SemaphoreType.DMA((slots,)),
            ],
        ),
        name="pack",
    )(position, blocks)


def swap_groups(parts, lane_group):
    for step in (4, 2, 1):
        low = (lane_group & step) == 0
        done = list(parts)
        for j in range(8):
            if j & step:
                continue
            a, b = parts[j], parts[j + step]
            done[j] = jnp.where(low, a, pltpu.roll(b, 16 * step, 1))
            done[j + step] = jnp.where(low, pltpu.roll(a, 128 - 16 * step, 1), b)
        parts = done
    return parts


def owner_kernel(
    sizes, valid, mu_of, nu_of, blocks, panel, metric, row_of, fitted_out, partial_out,
    held, acc, weights, xs, ys, fitted, in_sem, out_sem,
):
    rows, nbasis, fb, ab, occ, rb = sizes
    nblk = nbasis // fb
    tiles = ab // 4
    wide = ab * occ

    def fetch(j):
        return pltpu.make_async_copy(blocks.at[j], held.at[j], in_sem.at[j])

    @pl.loop(0, rows)
    def _(j):
        @pl.when(valid[j] > 0)
        def _():
            fetch(j).start()

    @pl.loop(0, nbasis // 8)
    def _(r):
        acc[pl.ds(pl.multiple_of(r * 8, 8), 8), :] = jnp.zeros((8, wide), F32)

    spread_row = iota((occ, 256), 0)
    spread_col = iota((occ, 256), 1)
    spread = ones_where((spread_col // 16) * 4 + spread_col % 4 == spread_row)
    same_q = iota((4 * fb, 256), 0) // fb == (iota((4 * fb, 256), 1) // 4) % 4

    @pl.loop(0, nblk)
    def _(n):
        part = panel[pl.ds(pl.multiple_of(n * fb, fb), fb), :]
        stacked = jnp.concatenate([part] * 4, axis=0)
        weights[n] = jnp.where(same_q, nn_dot(stacked, spread), 0.0).astype(BF)

    @pl.loop(0, rows)
    def _(j):
        @pl.when(valid[j] > 0)
        def _():
            fetch(j).wait()
            block = held[j]
            lhs = jnp.concatenate(
                [block[:, c * 128 : (c + 1) * 128] for c in range(tiles)], axis=0
            )
            half = nn_dot(lhs, weights[nu_of[j]]).astype(BF).astype(F32)
            at = pl.ds(pl.multiple_of(mu_of[j] * fb, fb), fb)
            for c in range(tiles):
                acc[at, c * 256 : (c + 1) * 256] += half[c * fb : (c + 1) * fb, :]

    expand = ones_where(iota((256, ab), 0) // 4 == iota((256, ab), 1))
    same_i = iota((256, 256), 0) % 4 == iota((256, 256), 1) % 4
    whole = metric[...]
    high = whole.astype(BF)
    low = (whole - high.astype(F32)).astype(BF)

    def widen(part):
        tall = nt_dot(expand, part).astype(BF)
        return jnp.where(same_i, nt_dot(tall, expand), 0.0).astype(BF)

    metric_high = widen(high)
    metric_low = widen(low)
    lane_from = iota((256, 256), 0)
    lane_to = iota((256, 256), 1)
    order = ones_where(
        ((lane_from // 4) % 4) * 64 + (lane_from // 16) * 4 + lane_from % 4 == lane_to
    )
    lane_group = iota((rb, 128), 1) // 16

    @pl.loop(0, nbasis // rb)
    def _(step):
        base = pl.multiple_of(step * rb, rb)
        at = pl.ds(base, rb)
        for ch in range(2):
            for h in range(2):
                parts = [
                    acc[at, (8 * ch + j) * 256 + h * 128 : (8 * ch + j) * 256 + h * 128 + 128]
                    for j in range(8)
                ]
                parts = swap_groups(parts, lane_group)
                for g in range(8):
                    xs[(8 * h + g) * rb : (8 * h + g + 1) * rb, ch * 128 : ch * 128 + 128] = parts[g]
        x = xs[...]
        x_high = x.astype(BF)
        x_low = (x - x_high.astype(F32)).astype(BF)
        y = nn_dot(x_high, metric_high) + nn_dot(x_low, metric_high) + nn_dot(x_high, metric_low)
        ys[...] = y.astype(BF).astype(F32)
        for ch in range(2):
            for h in range(2):
                parts = [
                    ys[(8 * ch + j) * rb : (8 * ch + j + 1) * rb, h * 128 : h * 128 + 128]
                    for j in range(8)
                ]
                parts = swap_groups(parts, lane_group)
                for g in range(8):
                    xs[(8 * h + g) * rb : (8 * h + g + 1) * rb, ch * 128 : ch * 128 + 128] = parts[g]
        f = nn_dot(xs[...].astype(BF), order).astype(BF)
        for c in range(tiles):
            fitted[at, c * 256 : (c + 1) * 256] = f[c * rb : (c + 1) * rb, :]
        pltpu.make_async_copy(fitted.at[at, :], fitted_out.at[at, :], out_sem.at[step]).start()

    total = jnp.zeros((nbasis, nbasis), F32)
    for k in range(wide // 512):
        part = fitted[:, k * 512 : (k + 1) * 512]
        total = total + nt_dot(part, part)
    pick = ones_where(row_of[...] == iota((nbasis, nbasis), 1))
    partial_out[...] = nn_dot(pick, total.astype(BF)).astype(BF)

    @pl.loop(0, nbasis // rb)
    def _(step):
        at = pl.ds(pl.multiple_of(step * rb, rb), rb)
        pltpu.make_async_copy(fitted.at[at, :], fitted_out.at[at, :], out_sem.at[step]).wait()


def owner(valid, mu_of, nu_of, blocks, panel, metric, row_of):
    rows, fb, inner = blocks.shape
    nbasis, occ = panel.shape
    ab = metric.shape[0]
    rb = 32
    wide = ab * occ
    vmem = pl.BlockSpec(memory_space=pltpu.VMEM)
    anywhere = pl.BlockSpec(memory_space=pl.ANY)
    return pl.pallas_call(
        functools.partial(owner_kernel, (rows, nbasis, fb, ab, occ, rb)),
        out_shape=(
            jax.ShapeDtypeStruct((nbasis, wide), BF),
            jax.ShapeDtypeStruct((nbasis, nbasis), BF),
        ),
        grid_spec=pltpu.PrefetchScalarGridSpec(
            num_scalar_prefetch=3,
            grid=(1,),
            in_specs=[anywhere, vmem, vmem, vmem],
            out_specs=(anywhere, vmem),
            scratch_shapes=[
                pltpu.VMEM((rows, fb, inner), BF),
                pltpu.VMEM((nbasis, wide), F32),
                pltpu.VMEM((nbasis // fb, 4 * fb, 256), BF),
                pltpu.VMEM((16 * rb, 256), F32),
                pltpu.VMEM((16 * rb, 256), F32),
                pltpu.VMEM((nbasis, wide), BF),
                pltpu.SemaphoreType.DMA((rows,)),
                pltpu.SemaphoreType.DMA((nbasis // rb,)),
            ],
        ),
        compiler_params=pltpu.CompilerParams(vmem_limit_bytes=48 << 20),
        name="owner",
    )(valid, mu_of, nu_of, blocks, panel, metric, row_of)


def shards(three_center, panel, metric, screen, pair_blocks):
    pair_count = lax.axis_size("pair")
    column_count = lax.axis_size("aux")
    own = lax.axis_index("pair")
    slots, fb, inner = three_center.shape
    ab = metric.shape[1]
    occ = panel.shape[1]
    nbasis = panel.shape[0] * pair_count
    capacity = 2
    targets = screen[:, :, 0]
    ids = jnp.arange(slots)
    earlier = ids[None, :] < ids[:, None]
    own_targets = lax.dynamic_index_in_dim(targets, own, 0, keepdims=False)
    own_ranks = jnp.sum(((own_targets[:, None] == own_targets[None, :]) & earlier).astype(jnp.int32), axis=1)
    position = own_targets * capacity + own_ranks
    outgoing = pack(position, three_center, pair_count * capacity)
    outgoing = outgoing.reshape(pair_count, capacity, fb, inner)

    whole_panel = lax.all_to_all(
        jnp.broadcast_to(panel[None], (pair_count,) + panel.shape), "pair", 0, 0, tiled=True
    ).reshape(nbasis, occ)
    arrived = lax.all_to_all(outgoing, "pair", 0, 0, tiled=True)

    mine = targets == own
    before = jnp.cumsum(mine.astype(jnp.int32), axis=1) - mine.astype(jnp.int32)
    hits = mine[:, None, :] & (before[:, None, :] == jnp.arange(capacity)[None, :, None])
    flat = pair_count * capacity
    valid = jnp.sum(hits.astype(jnp.int32), axis=2).reshape(flat)
    mu_of = jnp.sum(jnp.where(hits, pair_blocks[:, None, :, 0], 0), axis=2).reshape(flat)
    nu_of = jnp.sum(jnp.where(hits, pair_blocks[:, None, :, 1], 0), axis=2).reshape(flat)

    share = nbasis // (pair_count * column_count)
    row_of = jnp.arange(nbasis).reshape(pair_count, column_count, share)
    row_of = row_of.transpose(1, 0, 2).reshape(nbasis, 1)
    fitted, partial = owner(
        valid, mu_of, nu_of, arrived.reshape(flat, fb, inner), whole_panel, metric[0], row_of
    )
    partial = lax.all_to_all(
        partial.reshape(column_count, nbasis // column_count, nbasis), "aux", 0, 0, tiled=True
    )
    partial = jnp.sum(partial.astype(F32), axis=0).reshape(pair_count, share, nbasis)
    partial = lax.all_to_all(partial, "pair", 0, 0, tiled=True)
    norm_factor = 1.0 / (pair_count * column_count * ab * occ)
    return (fitted[None], jnp.sum(partial, axis=0) * norm_factor)


def solution(mesh):
    return jax.shard_map(
        shards,
        mesh=mesh,
        in_specs=(
            P(("pair", "aux"), None, None),
            P("pair", None),
            P(("pair", "aux"), None, None),
            P(None, "aux", None),
            P(None, "aux", None),
        ),
        out_specs=(P(("pair", "aux"), None, None), P(("pair", "aux"), None)),
        check_vma=False,
    )
```

time: 887 us -> 294 us (0.33)
  waiting for transfers between devices: 614 us -> 185 us
  local copies, waits for them, and re-layouts: 139 us -> 3.07 us
  matrix products: 58.6 us -> 0 us
  Pallas kernels: 0 us -> 41.6 us
  between operations: 14.1 us -> 0.74 us
  starting transfers between devices: 7.13 us -> 19.5 us
    unnamed x2 -> x0, waiting for transfers between devices: 260 us -> none
    all_to_all x1 -> x2, waiting for transfers between devices: 354 us -> 185 us  [the longest x1 183 us: shards(): arrived = lax.all_to_all(outgoing, 'pair', 0, 0, tiled=True)]
    reshape x8 -> x5, local copies, waits for them, and re-layouts: 100 us -> 0.5 us  [the longest x1 0.11 us: shards(): valid = jnp.sum(hits.astype(jnp.int32), axis=2).reshape(flat)]
    dot_general x6 -> x0, matrix products: 58.6 us -> none  [the longest x1 21.9 us: shards(): jnp.einsum('smqn,sni->smqi', blocks_local, own_panel, preferred_element_t...]
    all_gather x1 -> x0, blocking collectives: 45.7 us -> none  [shards(): whole_panel = lax.all_gather(panel, 'pair', axis=0, tiled=True)]
    pallas_call x0 -> x2, Pallas kernels: none -> 41.6 us  [the longest x1 36.5 us: owner(): pl.pallas_call(functools.partial(owner_kernel, (rows, nbasis, fb, ab, occ...]
    all_to_all x0 -> x2, blocking collectives: none -> 39 us  [the longest x1 23.8 us: shards(): partial = lax.all_to_all(partial, 'pair', 0, 0, tiled=True)]
    convert_element_type x2 -> x0, local copies, waits for them, and re-layouts: 29 us -> none  [the longest x1 22.5 us: shards(): transformed.astype(jnp.bfloat16).reshape(slot_count, block_size)]
  transfers between devices with their start and end apart: 2 -> 2, of which waited for: 2 -> 2; matrix products, arithmetic and copies ran while one was open for 2% -> 1% of each run, Pallas kernels for 0% -> 2%
where the time goes in v1:
time: 294 us; the launch traced here: 292 us
  waiting for transfers between devices  185 us (63%)
  Pallas kernels  41.6 us (14%)
  blocking collectives  39 us (13%)
  starting transfers between devices  19.5 us (7%)
  local copies, waits for them, and re-layouts  3.07 us (1%)
    all_to_all x1, waiting for transfers between devices, shards(): arrived = lax.all_to_all(outgoing, 'pair', 0, 0, tiled=True)  183 us
    pallas_call x1, Pallas kernels, owner(): pl.pallas_call(functools.partial(owner_kernel, (rows, nbasis, fb, ab, occ...  36.5 us
    all_to_all x1, blocking collectives, shards(): partial = lax.all_to_all(partial, 'pair', 0, 0, tiled=True)  23.8 us
    all_to_all x1, blocking collectives, shards(): lax.all_to_all(partial.reshape(column_count, nbasis // column_count, nbas...  15.3 us
    all_to_all x1, starting transfers between devices, shards(): lax.all_to_all(jnp.broadcast_to(panel[None], (pair_count,) + panel.shape)...  11.4 us
    all_to_all x1, starting transfers between devices, shards(): arrived = lax.all_to_all(outgoing, 'pair', 0, 0, tiled=True)  8.15 us
  transfers between devices with their start and end apart: 2, of which 2 were waited for; matrix products, arithmetic and copies ran while one was open for 1% of the time, Pallas kernels for 2%

profile of v1, /device:TPU:32, one launch (start us, length us, event | category | flops | bytes accessed | tf_op | source)
XLA Modules:
  0.0 291.6 jit_solution(15984738966457689470)
XLA Ops:
  0.6 0.7 broadcast_in_dim.43
  1.3 0.8 reshape.142
  2.1 11.4 %all-to-all-start.1 = ((bf16[32,2,512]{2,1,0:T(2,128)(2,1)}), bf16[32,2,512]{2,1,0:T(2,128)(2,1)S(1)}, u32[]{:S(2)}, u32[]{:S(2)}) async-start(bf16[32,2,512]{2,1,0:T(2,128)(2,1)} %reshape.142), calls=%async_computation.1 | async-start | bytes 131072 | tf_op jit(solution)/shard_map/all_to_all | solution.py:248
  13.5 0.7 dynamic-slice_bitcast_fusion
  14.1 0.2 convert_reduce_fusion.2
  14.3 1.2 multiply_add_fusion.1.position
  15.5 5.2 %pack.1 = bf16[64,32,2048]{2,1,0:T(8,128)(2,1)} custom-call(s32[32]{0:T(128)} %multiply_add_fusion.1.position, bf16[32,32,2048]{2,1,0:T(8,128)(2,1)} %blocks.1), custom_call_target="tpu_custom_call" | custom-call | tf_op jit(solution)/shard_map/pack/pallas_call | solution.py:52
  20.7 1.9 all-to-all-done.1
  22.6 0.0 copy-start.2
  22.6 0.0 copy-start.1
  22.6 0.0 copy-start
  22.6 8.1 %all-to-all-start = ((bf16[32,2,32,2048]{3,2,1,0:T(8,128)(2,1)}), bf16[32,2,32,2048]{3,2,1,0:T(8,128)(2,1)}, u32[]{:S(2)}, u32[]{:S(2)}) async-start(bf16[32,2,32,2048]{3,2,1,0:T(8,128)(2,1)} %bitcast.19), calls=%async_computation | async-start | bytes 16777216 | tf_op jit(solution)/shard_map/all_to_all | solution.py:251
  30.7 0.0 copy-done.2
  30.8 0.2 reduce_window_sum.11
  30.9 0.0 copy-done.1
  31.0 0.2 select_reduce_fusion
  31.2 0.1 copy.16
  31.3 0.1 reshape.120.valid
  31.4 0.1 copy.17
  31.5 0.1 reshape.121.mu_of
  31.6 0.1 copy.18
  31.7 0.1 reshape.122.nu_of
  31.8 0.1 reshape.135.row_of
  31.9 0.1 reshape.143
  32.1 183.2 %all-to-all-done = bf16[32,2,32,2048]{3,2,1,0:T(8,128)(2,1)} async-done(((bf16[32,2,32,2048]{3,2,1,0:T(8,128)(2,1)}), bf16[32,2,32,2048]{3,2,1,0:T(8,128)(2,1)}, u32[]{:S(2)}, u32[]{:S(2)}) %all-to-all-start) | async-done | bytes 8388640 | tf_op jit(solution)/shard_map/all_to_all | solution.py:251
  215.2 0.0 copy-done
  215.2 36.5 %owner.1 = (bf16[512,4096]{1,0:T(8,128)(2,1)}, bf16[512,512]{1,0:T(8,128)(2,1)S(1)}) custom-call(s32[64]{0:T(128)S(1)} %reshape.120.valid, s32[64]{0:T(128)S(1)} %reshape.121.mu_of, s32[64]{0:T(128)S(1)} %reshape.122.nu_of, bf16[64,32,2048]{2,1,0:T(8,128)(2,1)} %bitcast.6.blocks, bf16[512,64]{1,0:T(8,128)(2,1)S(1)} %bitcast.16, f32[64,64]{1,0:T(8,128)S(1)} %bitcast.18, ...), custom_call_target="tpu_custom_call" | custom-call | tf_op jit(solution)/shard_map/owner/pallas_call | solution.py:203
  251.7 15.3 %all_to_all.20 = bf16[8,64,512]{2,1,0:T(8,128)(2,1)S(1)} all-to-all(bf16[8,64,512]{2,1,0:T(8,128)(2,1)S(1)} %bitcast.17), channel_id=1, replica_groups=mesh['pair'=32,'aux'=8] {'aux'}, dimensions={0} | all-to-all | bytes 1048576 | tf_op jit(solution)/shard_map/all_to_all | solution.py:267
  267.0 0.1 convert_reduce_fusion
  267.1 0.1 reshape.134
  267.1 23.8 %all_to_all.21 = f32[32,2,512]{2,1,0:T(2,128)S(1)} all-to-all(f32[32,2,512]{2,1,0:T(2,128)S(1)} %reshape.134), channel_id=1, replica_groups=mesh['pair'=32,'aux'=8] {'pair'}, dimensions={0} | all-to-all | bytes 262144 | tf_op jit(solution)/shard_map/all_to_all | solution.py:271
  290.9 0.1 reduce_sum.59
  291.0 0.6 broadcast_multiply_fusion
  (4 shorter events, 0.1 us)
Async XLA Ops:
  2.1 20.5 %all-to-all-start.1 = ((bf16[32,2,512]{2,1,0:T(2,128)(2,1)}), bf16[32,2,512]{2,1,0:T(2,128)(2,1)S(1)}, u32[]{:S(2)}, u32[]{:S(2)}) async-start(bf16[32,2,512]{2,1,0:T(2,128)(2,1)} %reshape.142), calls=%async_computation.1 | async-start | bytes 131072 | tf_op jit(solution)/shard_map/all_to_all | solution.py:248
  22.6 8.2 %copy-start.2 = (s32[32,32,1]{1,2,0:T(1,128)S(1)}, s32[32,32,1]{1,2,0:T(1,128)}, u32[]{:S(2)}) copy-start(s32[32,32,1]{1,2,0:T(1,128)} %param.8) | copy-start | bytes 12292
  22.6 8.4 %copy-start.1 = (s32[32,32,2]{1,2,0:T(2,128)S(1)}, s32[32,32,2]{1,2,0:T(2,128)}, u32[]{:S(2)}) copy-start(s32[32,32,2]{1,2,0:T(2,128)} %param.9) | copy-start | bytes 24580
  22.6 192.7 %copy-start = (f32[1,64,64]{2,1,0:T(8,128)S(1)}, f32[1,64,64]{2,1,0:T(8,128)}, u32[]{:S(2)}) copy-start(f32[1,64,64]{2,1,0:T(8,128)} %param.7) | copy-start | bytes 49156
  22.6 192.7 %all-to-all-start = ((bf16[32,2,32,2048]{3,2,1,0:T(8,128)(2,1)}), bf16[32,2,32,2048]{3,2,1,0:T(8,128)(2,1)}, u32[]{:S(2)}, u32[]{:S(2)}) async-start(bf16[32,2,32,2048]{3,2,1,0:T(8,128)(2,1)} %bitcast.19), calls=%async_computation | async-start | bytes 16777216 | tf_op jit(solution)/shard_map/all_to_all | solution.py:251

commit v2 on v1

v2 whole, which is shorter than its diff:
```python
import functools
import jax
import jax.numpy as jnp
from jax import lax
from jax.experimental import pallas as pl
from jax.experimental.pallas import tpu as pltpu
from jax.sharding import PartitionSpec as P

BF = jnp.bfloat16
F32 = jnp.float32
SUBS = 4
YT = jnp.float32


def iota(shape, dim):
    return lax.broadcasted_iota(jnp.int32, shape, dim)


def ones_where(mask):
    return jnp.where(mask, 1.0, 0.0).astype(BF)


def nt_dot(a, b):
    return lax.dot_general(a, b, (((1,), (1,)), ((), ())), preferred_element_type=F32)


def nn_dot(a, b):
    return jnp.dot(a, b, preferred_element_type=F32)


def pack_kernel(sizes, target, blocks, panel, out, held, flat, seen, in_sem, out_sem, panel_sem):
    slots, owners, capacity = sizes
    fb = held.shape[1]
    tiles = held.shape[2] // 128
    length = flat.shape[1]

    def fetch(s):
        return pltpu.make_async_copy(blocks.at[s], held.at[s], in_sem.at[s])

    def put(s, rank):
        at = pl.ds(pl.multiple_of(rank * length, length), length)
        return pltpu.make_async_copy(flat.at[s], out.at[target[s], at, :], out_sem.at[s])

    def put_panel(p):
        return pltpu.make_async_copy(
            panel, out.at[p, pl.ds(capacity * length, panel.shape[0]), :], panel_sem.at[p]
        )

    @pl.loop(0, slots)
    def _(s):
        fetch(s).start()

    @pl.loop(0, owners)
    def _(p):
        put_panel(p).start()
        seen[p] = 0

    @pl.loop(0, slots)
    def _(s):
        fetch(s).wait()
        for c in range(tiles):
            row = (c % 2) * (length // 2) + (c // 2) * fb
            flat[s, row : row + fb, :] = held[s, :, c * 128 : (c + 1) * 128]
        rank = seen[target[s]]
        seen[target[s]] = rank + 1
        put(s, rank).start()

    @pl.loop(0, slots)
    def _(s):
        put(s, 0).wait()

    @pl.loop(0, owners)
    def _(p):
        put_panel(p).wait()


def pack(target, blocks, panel, owners, capacity):
    slots, fb, inner = blocks.shape
    length = fb * inner // 128
    return pl.pallas_call(
        functools.partial(pack_kernel, (slots, owners, capacity)),
        out_shape=jax.ShapeDtypeStruct((owners, capacity * length + panel.shape[0], 128), blocks.dtype),
        grid_spec=pltpu.PrefetchScalarGridSpec(
            num_scalar_prefetch=1,
            grid=(1,),
            in_specs=[pl.BlockSpec(memory_space=pl.ANY), pl.BlockSpec(memory_space=pltpu.VMEM)],
            out_specs=pl.BlockSpec(memory_space=pl.ANY),
            scratch_shapes=[
                pltpu.VMEM((slots, fb, inner), blocks.dtype),
                pltpu.VMEM((slots, length, 128), blocks.dtype),
                pltpu.SMEM((owners,), jnp.int32),
                pltpu.SemaphoreType.DMA((slots,)),
                pltpu.SemaphoreType.DMA((slots,)),
                pltpu.SemaphoreType.DMA((owners,)),
            ],
        ),
        compiler_params=pltpu.CompilerParams(vmem_limit_bytes=60 << 20),
        name="pack",
    )(target, blocks, panel)


def swap_groups(parts):
    count = len(parts)
    group = 128 // count
    lane_group = iota(parts[0].shape, 1) // group
    step = count // 2
    while step:
        low = (lane_group & step) == 0
        done = list(parts)
        for j in range(count):
            if j & step:
                continue
            a, b = parts[j], parts[j + step]
            done[j] = jnp.where(low, a, pltpu.roll(b, group * step, 1))
            done[j + step] = jnp.where(low, pltpu.roll(a, 128 - group * step, 1), b)
        parts = done
        step //= 2
    return parts


def owner_kernel(
    sizes, valid, mu_of, nu_of, arrived, metric, row_of, fitted_out, partial_out,
    held, panel, acc, weights, xs_all, ys_all, zs_all, fitted, total, in_sem, out_sem, panel_sem,
):
    rows, nbasis, fb, ab, occ, rb, capacity = sizes
    length = held.shape[1]
    nblk = nbasis // fb
    tiles = ab // 4
    wide = ab * occ

    def fetch(j):
        at = pl.ds(pl.multiple_of(lax.rem(j, capacity) * length, length), length)
        return pltpu.make_async_copy(arrived.at[lax.div(j, capacity), at, :], held.at[j], in_sem.at[j])

    fetch_panel = pltpu.make_async_copy(
        arrived.at[:, pl.ds(capacity * length, panel.shape[1]), :], panel, panel_sem
    )
    fetch_panel.start()

    @pl.loop(0, rows)
    def _(j):
        @pl.when(valid[j] > 0)
        def _():
            fetch(j).start()

    @pl.loop(0, nbasis // 8)
    def _(r):
        acc[pl.ds(pl.multiple_of(r * 8, 8), 8), :] = jnp.zeros((8, wide), F32)

    pick_row = iota((8 * fb, fb // 2), 0) % fb // 2 == iota((8 * fb, fb // 2), 1)
    same_half = iota((8 * fb, 128), 0) % 2 == iota((8 * fb, 128), 1) // occ
    spread_row = iota((128, 512), 0) % occ
    spread_col = iota((128, 512), 1)
    spread = ones_where((spread_col // 32) * 4 + spread_col % 4 == spread_row)
    same_q = iota((8 * fb, 512), 0) // fb == (iota((8 * fb, 512), 1) // 4) % 8
    pick_row = ones_where(pick_row)
    per_block = fb // 2 // panel.shape[1]
    fetch_panel.wait()

    @pl.loop(0, nblk)
    def _(n):
        part = jnp.concatenate([panel[n * per_block + k].astype(F32) for k in range(per_block)], axis=0)
        tall = jnp.where(same_half, nn_dot(pick_row, part.astype(BF)), 0.0).astype(BF)
        weights[n] = jnp.where(same_q, nn_dot(tall, spread), 0.0).astype(BF)

    @pl.loop(0, rows)
    def _(j):
        @pl.when(valid[j] > 0)
        def _():
            fetch(j).wait()
            block = held[j]
            lhs = jnp.concatenate([block[: length // 2], block[length // 2 :]], axis=1)
            half = nn_dot(lhs, weights[nu_of[j]])
            at = pl.ds(pl.multiple_of(mu_of[j] * fb, fb), fb)
            for c in range(tiles // 2):
                acc[at, c * 512 : (c + 1) * 512] += half[c * fb : (c + 1) * fb, :]

    expand = ones_where(iota((256, ab), 0) // 4 == iota((256, ab), 1))
    same_i = iota((256, 256), 0) % 4 == iota((256, 256), 1) % 4
    whole = metric[...]
    high = whole.astype(BF)
    low = (whole - high.astype(F32)).astype(BF)

    def widen(part):
        tall = nt_dot(expand, part).astype(BF)
        return jnp.where(same_i, nt_dot(tall, expand), 0.0).astype(BF)

    metric_high = widen(high)
    metric_low = widen(low)
    lane_from = iota((256, 256), 0)
    lane_to = iota((256, 256), 1)
    order = ones_where(
        ((lane_from // 4) % 4) * 64 + (lane_from // 16) * 4 + lane_from % 4 == lane_to
    )

    @pl.loop(0, nbasis // (SUBS * rb))
    def _(step):
        for sub in range(SUBS):
            xs, ys, zs = xs_all[sub], ys_all[sub], zs_all[sub]
            place = step * SUBS + sub
            at = pl.ds(pl.multiple_of(place * rb, rb), rb)
            for v in range(4):
                for ch in range(2):
                    parts = [
                        acc[at, (4 * ch + j) * 512 + v * 128 : (4 * ch + j) * 512 + v * 128 + 128]
                        for j in range(4)
                    ]
                    parts = swap_groups(parts)
                    for g in range(4):
                        xs[(4 * v + g) * rb : (4 * v + g + 1) * rb, ch * 128 : ch * 128 + 128] = parts[g]
            x = xs[...]
            x_high = x.astype(BF)
            x_low = (x - x_high.astype(F32)).astype(BF)
            y = nn_dot(x_high, metric_high) + nn_dot(x_low, metric_high) + nn_dot(x_high, metric_low)
            ys[...] = y.astype(BF).astype(YT)
            for ch in range(2):
                for h in range(2):
                    parts = [
                        ys[(8 * ch + j) * rb : (8 * ch + j + 1) * rb, h * 128 : h * 128 + 128]
                        for j in range(8)
                    ]
                    parts = swap_groups(parts)
                    for g in range(8):
                        zs[(8 * h + g) * rb : (8 * h + g + 1) * rb, ch * 128 : ch * 128 + 128] = parts[g].astype(BF)
            f = nn_dot(zs[...], order).astype(BF)
            for c in range(tiles):
                fitted[at, c * 256 : (c + 1) * 256] = f[c * rb : (c + 1) * rb, :]
            pltpu.make_async_copy(fitted.at[at, :], fitted_out.at[at, :], out_sem.at[place]).start()

    total[...] = jnp.zeros((nbasis, nbasis), F32)

    @pl.loop(0, wide // 1024)
    def _(k):
        part = fitted[:, pl.ds(pl.multiple_of(k * 1024, 1024), 1024)]
        total[...] += nt_dot(part, part)

    pick = ones_where(row_of[...] == iota((nbasis, nbasis), 1))
    partial_out[...] = nn_dot(pick, total[...].astype(BF)).astype(BF)

    @pl.loop(0, nbasis // rb)
    def _(step):
        at = pl.ds(pl.multiple_of(step * rb, rb), rb)
        pltpu.make_async_copy(fitted.at[at, :], fitted_out.at[at, :], out_sem.at[step]).wait()


def owner(valid, mu_of, nu_of, arrived, metric, row_of, fb, occ):
    rows = valid.shape[0]
    owners = arrived.shape[0]
    capacity = rows // owners
    nbasis = row_of.shape[0]
    ab = metric.shape[0]
    length = fb * ab * fb // 128
    rb = 32
    wide = ab * occ
    vmem = pl.BlockSpec(memory_space=pltpu.VMEM)
    anywhere = pl.BlockSpec(memory_space=pl.ANY)
    return pl.pallas_call(
        functools.partial(owner_kernel, (rows, nbasis, fb, ab, occ, rb, capacity)),
        out_shape=(
            jax.ShapeDtypeStruct((nbasis, wide), BF),
            jax.ShapeDtypeStruct((nbasis, nbasis), BF),
        ),
        grid_spec=pltpu.PrefetchScalarGridSpec(
            num_scalar_prefetch=3,
            grid=(1,),
            in_specs=[anywhere, vmem, vmem],
            out_specs=(anywhere, vmem),
            scratch_shapes=[
                pltpu.VMEM((rows, length, 128), BF),
                pltpu.VMEM((owners, arrived.shape[1] - capacity * length, 128), BF),
                pltpu.VMEM((nbasis, wide), F32),
                pltpu.VMEM((nbasis // fb, 8 * fb, 512), BF),
                [pltpu.VMEM((16 * rb, 256), F32)] * SUBS,
                [pltpu.VMEM((16 * rb, 256), YT)] * SUBS,
                [pltpu.VMEM((16 * rb, 256), BF)] * SUBS,
                pltpu.VMEM((nbasis, wide), BF),
                pltpu.VMEM((nbasis, nbasis), F32),
                pltpu.SemaphoreType.DMA((rows,)),
                pltpu.SemaphoreType.DMA((nbasis // rb,)),
                pltpu.SemaphoreType.DMA,
            ],
        ),
        compiler_params=pltpu.CompilerParams(vmem_limit_bytes=60 << 20),
        name="owner",
    )(valid, mu_of, nu_of, arrived, metric, row_of)


def shards(three_center, panel, metric, screen, pair_blocks):
    pair_count = lax.axis_size("pair")
    column_count = lax.axis_size("aux")
    own = lax.axis_index("pair")
    slots, fb, inner = three_center.shape
    ab = metric.shape[1]
    occ = panel.shape[1]
    nbasis = panel.shape[0] * pair_count
    capacity = 2
    targets = screen[:, :, 0]
    own_targets = lax.dynamic_index_in_dim(targets, own, 0, keepdims=False)
    outgoing = pack(own_targets, three_center, panel.reshape(-1, 128), pair_count, capacity)
    arrived = lax.all_to_all(outgoing, "pair", 0, 0, tiled=True)

    mine = targets == own
    before = jnp.cumsum(mine.astype(jnp.int32), axis=1) - mine.astype(jnp.int32)
    hits = mine[:, None, :] & (before[:, None, :] == jnp.arange(capacity)[None, :, None])
    flat = pair_count * capacity
    valid = jnp.sum(hits.astype(jnp.int32), axis=2).reshape(flat)
    mu_of = jnp.sum(jnp.where(hits, pair_blocks[:, None, :, 0], 0), axis=2).reshape(flat)
    nu_of = jnp.sum(jnp.where(hits, pair_blocks[:, None, :, 1], 0), axis=2).reshape(flat)

    share = nbasis // (pair_count * column_count)
    row_of = jnp.arange(nbasis).reshape(pair_count, column_count, share)
    row_of = row_of.transpose(1, 0, 2).reshape(nbasis, 1)
    fitted, partial = owner(valid, mu_of, nu_of, arrived, metric[0], row_of, fb, occ)
    partial = lax.all_to_all(
        partial.reshape(column_count, nbasis // column_count, nbasis), "aux", 0, 0, tiled=True
    )
    partial = jnp.sum(partial.astype(F32), axis=0).reshape(pair_count, share, nbasis)
    partial = lax.all_to_all(partial, "pair", 0, 0, tiled=True)
    norm_factor = 1.0 / (pair_count * column_count * ab * occ)
    return (fitted[None], jnp.sum(partial, axis=0) * norm_factor)


def solution(mesh):
    return jax.shard_map(
        shards,
        mesh=mesh,
        in_specs=(
            P(("pair", "aux"), None, None),
            P("pair", None),
            P(("pair", "aux"), None, None),
            P(None, "aux", None),
            P(None, "aux", None),
        ),
        out_specs=(P(("pair", "aux"), None, None), P(("pair", "aux"), None)),
        check_vma=False,
    )
```

time: 294 us -> 290 us (0.986)
  starting transfers between devices: 19.5 us -> 11.4 us
  waiting for transfers between devices: 185 us -> 189 us
    all_to_all x1 -> x0, starting transfers between devices: 11.4 us -> none  [shards(): lax.all_to_all(jnp.broadcast_to(panel[None], (pair_count,) + panel.shape)...]
    all_to_all x1, waiting for transfers between devices: 183 us -> 189 us  [shards(): arrived = lax.all_to_all(outgoing, 'pair', 0, 0, tiled=True)]
    all_to_all x1, starting transfers between devices: 8.15 us -> 11.4 us  [shards(): arrived = lax.all_to_all(outgoing, 'pair', 0, 0, tiled=True)]
  transfers between devices with their start and end apart: 2 -> 1, of which waited for: 2 -> 1; matrix products, arithmetic and copies ran while one was open for 1% -> 1% of each run, Pallas kernels for 2% -> 0%
where the time goes in v2:
time: 290 us
  waiting for transfers between devices  189 us (65%)
  Pallas kernels  43.3 us (15%)
  blocking collectives  38.8 us (13%)
  starting transfers between devices  11.4 us (4%)
  local copies, waits for them, and re-layouts  5.62 us (2%)
    all_to_all x1, waiting for transfers between devices, shards(): arrived = lax.all_to_all(outgoing, 'pair', 0, 0, tiled=True)  189 us
    pallas_call x1, Pallas kernels, owner(): pl.pallas_call(functools.partial(owner_kernel, (rows, nbasis, fb, ab, occ...  36.9 us
    all_to_all x1, blocking collectives, shards(): partial = lax.all_to_all(partial, 'pair', 0, 0, tiled=True)  24.8 us
    all_to_all x1, blocking collectives, shards(): lax.all_to_all(partial.reshape(column_count, nbasis // column_count, nbas...  14 us
    all_to_all x1, starting transfers between devices, shards(): arrived = lax.all_to_all(outgoing, 'pair', 0, 0, tiled=True)  11.4 us
    pallas_call x1, Pallas kernels, pack(): pl.pallas_call(functools.partial(pack_kernel, (slots, owners, capacity)),...  6.39 us
  transfers between devices with their start and end apart: 1, of which 1 were waited for; matrix products, arithmetic and copies ran while one was open for 1% of the time, Pallas kernels for 0%

profile of v2, /device:TPU:32, one launch (start us, length us, event | category | flops | bytes accessed | tf_op | source)
XLA Modules:
  0.0 290.1 jit_solution(2887900310021881854)
XLA Ops:
  0.6 1.3 reshape.113.panel
  2.0 1.2 dynamic-slice_bitcast_fusion.target
  3.1 6.4 %pack.1 = bf16[32,1032,128]{2,1,0:T(8,128)(2,1)} custom-call(s32[32]{0:T(128)} %dynamic-slice_bitcast_fusion.target, bf16[32,32,2048]{2,1,0:T(8,128)(2,1)} %blocks.1, bf16[8,128]{1,0:T(8,128)(2,1)} %reshape.113.panel), custom_call_target="tpu_custom_call" | custom-call | tf_op jit(solution)/shard_map/pack/pallas_call | solution.py:80
  9.5 0.0 copy-start.1
  9.6 0.0 copy-start
  9.6 11.4 %all-to-all-start = ((bf16[32,1032,128]{2,1,0:T(8,128)(2,1)}), bf16[32,1032,128]{2,1,0:T(8,128)(2,1)}, u32[]{:S(2)}, u32[]{:S(2)}) async-start(bf16[32,1032,128]{2,1,0:T(8,128)(2,1)} %pack.1), calls=%async_computation | async-start | bytes 16908288 | tf_op jit(solution)/shard_map/all_to_all | solution.py:300
  21.0 0.0 copy-done.1
  21.0 0.2 reduce_window_sum.11
  21.2 0.0 copy-done
  21.2 0.2 select_reduce_fusion
  21.4 0.1 copy.16
  21.5 0.6 reshape.110.valid
  22.2 0.1 copy.17
  22.2 0.6 reshape.111.mu_of
  22.9 0.1 copy.18
  23.0 0.7 reshape.112.nu_of
  23.6 0.8 reshape.123.row_of
  24.4 189.1 %all-to-all-done.arrived = bf16[32,1032,128]{2,1,0:T(8,128)(2,1)} async-done(((bf16[32,1032,128]{2,1,0:T(8,128)(2,1)}), bf16[32,1032,128]{2,1,0:T(8,128)(2,1)}, u32[]{:S(2)}, u32[]{:S(2)}) %all-to-all-start) | async-done | bytes 8454176 | tf_op jit(solution)/shard_map/all_to_all | solution.py:300
  213.6 36.9 %owner.1 = (bf16[512,4096]{1,0:T(8,128)(2,1)}, bf16[512,512]{1,0:T(8,128)(2,1)}) custom-call(s32[64]{0:T(128)} %reshape.110.valid, s32[64]{0:T(128)} %reshape.111.mu_of, s32[64]{0:T(128)} %reshape.112.nu_of, bf16[32,1032,128]{2,1,0:T(8,128)(2,1)} %all-to-all-done.arrived, f32[64,64]{1,0:T(8,128)} %bitcast.14, s32[512,1]{1,0:T(8,128)} %reshape.123.row_of), custom_call_target="tpu_custom_call" | custom-call | tf_op jit(solution)/shard_map/owner/pallas_call | solution.py:257
  250.5 14.0 %all_to_all.15 = bf16[8,64,512]{2,1,0:T(8,128)(2,1)S(1)} all-to-all(bf16[8,64,512]{2,1,0:T(8,128)(2,1)} %bitcast.11), channel_id=1, replica_groups=mesh['pair'=32,'aux'=8] {'aux'}, dimensions={0} | all-to-all | bytes 1048576 | tf_op jit(solution)/shard_map/all_to_all | solution.py:314
  264.5 0.1 convert_reduce_fusion
  264.5 0.1 reshape.122
  264.6 24.8 %all_to_all.16 = f32[32,2,512]{2,1,0:T(2,128)S(1)} all-to-all(f32[32,2,512]{2,1,0:T(2,128)S(1)} %reshape.122), channel_id=1, replica_groups=mesh['pair'=32,'aux'=8] {'pair'}, dimensions={0} | all-to-all | bytes 262144 | tf_op jit(solution)/shard_map/all_to_all | solution.py:318
  289.5 0.1 reduce_sum.49
  289.5 0.6 broadcast_multiply_fusion
  (4 shorter events, 0.1 us)
Async XLA Ops:
  9.5 11.4 %copy-start.1 = (s32[32,32,1]{1,2,0:T(1,128)S(1)}, s32[32,32,1]{1,2,0:T(1,128)}, u32[]{:S(2)}) copy-start(s32[32,32,1]{1,2,0:T(1,128)} %param.8) | copy-start | bytes 12292
  9.6 11.7 %copy-start = (s32[32,32,2]{1,2,0:T(2,128)S(1)}, s32[32,32,2]{1,2,0:T(2,128)}, u32[]{:S(2)}) copy-start(s32[32,32,2]{1,2,0:T(2,128)} %param.9) | copy-start | bytes 24580
  9.6 204.0 %all-to-all-start = ((bf16[32,1032,128]{2,1,0:T(8,128)(2,1)}), bf16[32,1032,128]{2,1,0:T(8,128)(2,1)}, u32[]{:S(2)}, u32[]{:S(2)}) async-start(bf16[32,1032,128]{2,1,0:T(8,128)(2,1)} %pack.1), calls=%async_computation | async-start | bytes 16908288 | tf_op jit(solution)/shard_map/all_to_all | solution.py:300

commit v3 on v2

--- a/solution.py
+++ b/solution.py
@@ -9,6 +9,8 @@
 BF = jnp.bfloat16
 F32 = jnp.float32
 SUBS = 4
+GROUP = 4
+WSTEP = 4
 YT = jnp.float32
 
 
@@ -120,7 +122,7 @@
 
 def owner_kernel(
     sizes, valid, mu_of, nu_of, arrived, metric, row_of, fitted_out, partial_out,
-    held, panel, acc, weights, xs_all, ys_all, zs_all, fitted, total, in_sem, out_sem, panel_sem,
+    held, panel, acc, weights, xs_all, ys_all, zs_all, fitted, total, listed, tally, in_sem, out_sem, panel_sem,
 ):
     rows, nbasis, fb, ab, occ, rb, capacity = sizes
     length = held.shape[1]
@@ -137,41 +139,67 @@
     )
     fetch_panel.start()
 
+    tally[0] = 0
+
+    @pl.loop(0, rows)
+    def _(j):
+        listed[j] = 0
+
     @pl.loop(0, rows)
     def _(j):
         @pl.when(valid[j] > 0)
         def _():
             fetch(j).start()
+            listed[tally[0]] = j
+            tally[0] = tally[0] + 1
+
+    count = tally[0]
 
     @pl.loop(0, nbasis // 8)
     def _(r):
         acc[pl.ds(pl.multiple_of(r * 8, 8), 8), :] = jnp.zeros((8, wide), F32)
 
-    pick_row = iota((8 * fb, fb // 2), 0) % fb // 2 == iota((8 * fb, fb // 2), 1)
-    same_half = iota((8 * fb, 128), 0) % 2 == iota((8 * fb, 128), 1) // occ
+    pick_row = ones_where(iota((fb, fb // 2), 0) // 2 == iota((fb, fb // 2), 1))
+    same_half = iota((fb, 128), 0) % 2 == iota((fb, 128), 1) // occ
     spread_row = iota((128, 512), 0) % occ
     spread_col = iota((128, 512), 1)
     spread = ones_where((spread_col // 32) * 4 + spread_col % 4 == spread_row)
-    same_q = iota((8 * fb, 512), 0) // fb == (iota((8 * fb, 512), 1) // 4) % 8
-    pick_row = ones_where(pick_row)
+    column_q = (iota((fb, 512), 1) // 4) % 8
     per_block = fb // 2 // panel.shape[1]
     fetch_panel.wait()
 
-    @pl.loop(0, nblk)
-    def _(n):
-        part = jnp.concatenate([panel[n * per_block + k].astype(F32) for k in range(per_block)], axis=0)
-        tall = jnp.where(same_half, nn_dot(pick_row, part.astype(BF)), 0.0).astype(BF)
-        weights[n] = jnp.where(same_q, nn_dot(tall, spread), 0.0).astype(BF)
-
-    @pl.loop(0, rows)
-    def _(j):
-        @pl.when(valid[j] > 0)
-        def _():
-            fetch(j).wait()
+    @pl.loop(0, nblk // WSTEP)
+    def _(step):
+        for k in range(WSTEP):
+            n = step * WSTEP + k
+            part = jnp.concatenate([panel[n * per_block + k].astype(F32) for k in range(per_block)], axis=0)
+            tall = jnp.where(same_half, nn_dot(pick_row, part.astype(BF)), 0.0).astype(BF)
+            broad = nn_dot(tall, spread)
+            for q in range(8):
+                weights[n, q * fb : (q + 1) * fb, :] = jnp.where(column_q == q, broad, 0.0).astype(BF)
+
+    held[rows] = jnp.zeros(held.shape[1:], BF)
+
+    @pl.loop(0, (count + GROUP - 1) // GROUP)
+    def _(step):
+        picks = []
+        for k in range(GROUP):
+            at = step * GROUP + k
+            there = at < count
+            j = listed[jnp.minimum(at, rows - 1)]
+
+            @pl.when(there)
+            def _():
+                fetch(j).wait()
+
+            picks.append((jnp.where(there, j, rows), jnp.where(there, mu_of[j], 0), jnp.where(there, nu_of[j], 0)))
+        halves = []
+        for j, mu, nu in picks:
             block = held[j]
             lhs = jnp.concatenate([block[: length // 2], block[length // 2 :]], axis=1)
-            half = nn_dot(lhs, weights[nu_of[j]])
-            at = pl.ds(pl.multiple_of(mu_of[j] * fb, fb), fb)
+            halves.append(nn_dot(lhs, weights[nu]))
+        for (j, mu, nu), half in zip(picks, halves):
+            at = pl.ds(pl.multiple_of(mu * fb, fb), fb)
             for c in range(tiles // 2):
                 acc[at, c * 512 : (c + 1) * 512] += half[c * fb : (c + 1) * fb, :]
 
@@ -187,6 +215,7 @@
 
     metric_high = widen(high)
     metric_low = widen(low)
+    metric_all = jnp.concatenate([metric_high, metric_high, metric_low], axis=0)
     lane_from = iota((256, 256), 0)
     lane_to = iota((256, 256), 1)
     order = ones_where(
@@ -211,7 +240,7 @@
             x = xs[...]
             x_high = x.astype(BF)
             x_low = (x - x_high.astype(F32)).astype(BF)
-            y = nn_dot(x_high, metric_high) + nn_dot(x_low, metric_high) + nn_dot(x_high, metric_low)
+            y = nn_dot(jnp.concatenate([x_high, x_low, x_high], axis=1), metric_all)
             ys[...] = y.astype(BF).astype(YT)
             for ch in range(2):
                 for h in range(2):
@@ -266,7 +295,7 @@
             in_specs=[anywhere, vmem, vmem],
             out_specs=(anywhere, vmem),
             scratch_shapes=[
-                pltpu.VMEM((rows, length, 128), BF),
+                pltpu.VMEM((rows + 1, length, 128), BF),
                 pltpu.VMEM((owners, arrived.shape[1] - capacity * length, 128), BF),
                 pltpu.VMEM((nbasis, wide), F32),
                 pltpu.VMEM((nbasis // fb, 8 * fb, 512), BF),
@@ -275,6 +304,8 @@
                 [pltpu.VMEM((16 * rb, 256), BF)] * SUBS,
                 pltpu.VMEM((nbasis, wide), BF),
                 pltpu.VMEM((nbasis, nbasis), F32),
+                pltpu.SMEM((rows,), jnp.int32),
+                pltpu.SMEM((1,), jnp.int32),
                 pltpu.SemaphoreType.DMA((rows,)),
                 pltpu.SemaphoreType.DMA((nbasis // rb,)),
                 pltpu.SemaphoreType.DMA,

time: 290 us -> 284 us (0.979)
  blocking collectives: 38.8 us -> 34.7 us
    all_to_all x1, blocking collectives: 24.8 us -> 18.7 us  [shards(): partial = lax.all_to_all(partial, 'pair', 0, 0, tiled=True)]
where the time goes in v3:
time: 284 us; the launch traced here: 283 us
  waiting for transfers between devices  188 us (66%)
  Pallas kernels  41.6 us (15%)
  blocking collectives  34.7 us (12%)
  starting transfers between devices  11.4 us (4%)
  local copies, waits for them, and re-layouts  5.62 us (2%)
    all_to_all x1, waiting for transfers between devices, shards(): arrived = lax.all_to_all(outgoing, 'pair', 0, 0, tiled=True)  188 us
    pallas_call x1, Pallas kernels, owner(): pl.pallas_call(functools.partial(owner_kernel, (rows, nbasis, fb, ab, occ...  35.2 us
    all_to_all x1, blocking collectives, shards(): partial = lax.all_to_all(partial, 'pair', 0, 0, tiled=True)  18.7 us
    all_to_all x1, blocking collectives, shards(): lax.all_to_all(partial.reshape(column_count, nbasis // column_count, nbas...  15.9 us
    all_to_all x1, starting transfers between devices, shards(): arrived = lax.all_to_all(outgoing, 'pair', 0, 0, tiled=True)  11.4 us
    pallas_call x1, Pallas kernels, pack(): pl.pallas_call(functools.partial(pack_kernel, (slots, owners, capacity)),...  6.37 us
  transfers between devices with their start and end apart: 1, of which 1 were waited for; matrix products, arithmetic and copies ran while one was open for 1% of the time, Pallas kernels for 0%

profile of v3, /device:TPU:32, one launch (start us, length us, event | category | flops | bytes accessed | tf_op | source)
XLA Modules:
  0.0 283.2 jit_solution(3682499271030865346)
XLA Ops:
  0.6 1.3 reshape.113.panel
  2.0 1.2 dynamic-slice_bitcast_fusion.target
  3.1 6.4 %pack.1 = bf16[32,1032,128]{2,1,0:T(8,128)(2,1)} custom-call(s32[32]{0:T(128)} %dynamic-slice_bitcast_fusion.target, bf16[32,32,2048]{2,1,0:T(8,128)(2,1)} %blocks.1, bf16[8,128]{1,0:T(8,128)(2,1)} %reshape.113.panel), custom_call_target="tpu_custom_call" | custom-call | tf_op jit(solution)/shard_map/pack/pallas_call | solution.py:82
  9.5 0.0 copy-start.1
  9.5 0.0 copy-start
  9.5 11.4 %all-to-all-start = ((bf16[32,1032,128]{2,1,0:T(8,128)(2,1)}), bf16[32,1032,128]{2,1,0:T(8,128)(2,1)}, u32[]{:S(2)}, u32[]{:S(2)}) async-start(bf16[32,1032,128]{2,1,0:T(8,128)(2,1)} %pack.1), calls=%async_computation | async-start | bytes 16908288 | tf_op jit(solution)/shard_map/all_to_all | solution.py:331
  21.0 0.0 copy-done.1
  21.0 0.2 reduce_window_sum.11
  21.2 0.0 copy-done
  21.3 0.2 select_reduce_fusion
  21.4 0.1 copy.16
  21.5 0.6 reshape.110.valid
  22.2 0.1 copy.17
  22.2 0.6 reshape.111.mu_of
  22.9 0.1 copy.18
  23.0 0.7 reshape.112.nu_of
  23.7 0.8 reshape.123.row_of
  24.5 188.1 %all-to-all-done.arrived = bf16[32,1032,128]{2,1,0:T(8,128)(2,1)} async-done(((bf16[32,1032,128]{2,1,0:T(8,128)(2,1)}), bf16[32,1032,128]{2,1,0:T(8,128)(2,1)}, u32[]{:S(2)}, u32[]{:S(2)}) %all-to-all-start) | async-done | bytes 8454176 | tf_op jit(solution)/shard_map/all_to_all | solution.py:331
  212.5 35.2 %owner.1 = (bf16[512,4096]{1,0:T(8,128)(2,1)}, bf16[512,512]{1,0:T(8,128)(2,1)}) custom-call(s32[64]{0:T(128)} %reshape.110.valid, s32[64]{0:T(128)} %reshape.111.mu_of, s32[64]{0:T(128)} %reshape.112.nu_of, bf16[32,1032,128]{2,1,0:T(8,128)(2,1)} %all-to-all-done.arrived, f32[64,64]{1,0:T(8,128)} %bitcast.14, s32[512,1]{1,0:T(8,128)} %reshape.123.row_of), custom_call_target="tpu_custom_call" | custom-call | tf_op jit(solution)/shard_map/owner/pallas_call | solution.py:286
  247.8 15.9 %all_to_all.15 = bf16[8,64,512]{2,1,0:T(8,128)(2,1)S(1)} all-to-all(bf16[8,64,512]{2,1,0:T(8,128)(2,1)} %bitcast.11), channel_id=1, replica_groups=mesh['pair'=32,'aux'=8] {'aux'}, dimensions={0} | all-to-all | bytes 1048576 | tf_op jit(solution)/shard_map/all_to_all | solution.py:345
  263.7 0.1 convert_reduce_fusion
  263.8 0.1 reshape.122
  263.8 18.7 %all_to_all.16 = f32[32,2,512]{2,1,0:T(2,128)S(1)} all-to-all(f32[32,2,512]{2,1,0:T(2,128)S(1)} %reshape.122), channel_id=1, replica_groups=mesh['pair'=32,'aux'=8] {'pair'}, dimensions={0} | all-to-all | bytes 262144 | tf_op jit(solution)/shard_map/all_to_all | solution.py:349
  282.6 0.1 reduce_sum.49
  282.6 0.6 broadcast_multiply_fusion
  (4 shorter events, 0.1 us)
Async XLA Ops:
  9.5 11.5 %copy-start.1 = (s32[32,32,1]{1,2,0:T(1,128)S(1)}, s32[32,32,1]{1,2,0:T(1,128)}, u32[]{:S(2)}) copy-start(s32[32,32,1]{1,2,0:T(1,128)} %param.8) | copy-start | bytes 12292
  9.5 11.7 %copy-start = (s32[32,32,2]{1,2,0:T(2,128)S(1)}, s32[32,32,2]{1,2,0:T(2,128)}, u32[]{:S(2)}) copy-start(s32[32,32,2]{1,2,0:T(2,128)} %param.9) | copy-start | bytes 24580
  9.5 203.0 %all-to-all-start = ((bf16[32,1032,128]{2,1,0:T(8,128)(2,1)}), bf16[32,1032,128]{2,1,0:T(8,128)(2,1)}, u32[]{:S(2)}, u32[]{:S(2)}) async-start(bf16[32,1032,128]{2,1,0:T(8,128)(2,1)} %pack.1), calls=%async_computation | async-start | bytes 16908288 | tf_op jit(solution)/shard_map/all_to_all | solution.py:331

commit v4 on v3

--- a/solution.py
+++ b/solution.py
@@ -121,10 +121,10 @@
 
 
 def owner_kernel(
-    sizes, valid, mu_of, nu_of, arrived, metric, row_of, fitted_out, partial_out,
+    sizes, number, arrived, metric, fitted_out, partial_out,
     held, panel, acc, weights, xs_all, ys_all, zs_all, fitted, total, listed, tally, in_sem, out_sem, panel_sem,
 ):
-    rows, nbasis, fb, ab, occ, rb, capacity = sizes
+    rows, nbasis, fb, ab, occ, rb, capacity, columns, share = sizes
     length = held.shape[1]
     nblk = nbasis // fb
     tiles = ab // 4
@@ -147,7 +147,7 @@
 
     @pl.loop(0, rows)
     def _(j):
-        @pl.when(valid[j] > 0)
+        @pl.when(number[j] > 0)
         def _():
             fetch(j).start()
             listed[tally[0]] = j
@@ -192,7 +192,8 @@
             def _():
                 fetch(j).wait()
 
-            picks.append((jnp.where(there, j, rows), jnp.where(there, mu_of[j], 0), jnp.where(there, nu_of[j], 0)))
+            pair = jnp.where(there, number[j] - 1, 0)
+            picks.append((jnp.where(there, j, rows), lax.div(pair, nblk), lax.rem(pair, nblk)))
         halves = []
         for j, mu, nu in picks:
             block = held[j]
@@ -263,7 +264,9 @@
         part = fitted[:, pl.ds(pl.multiple_of(k * 1024, 1024), 1024)]
         total[...] += nt_dot(part, part)
 
-    pick = ones_where(row_of[...] == iota((nbasis, nbasis), 1))
+    order_row = iota((nbasis, nbasis), 0)
+    column, pair, e = order_row // (nbasis // columns), order_row // share % (nbasis // columns // share), order_row % share
+    pick = ones_where((pair * columns + column) * share + e == iota((nbasis, nbasis), 1))
     partial_out[...] = nn_dot(pick, total[...].astype(BF)).astype(BF)
 
     @pl.loop(0, nbasis // rb)
@@ -272,11 +275,10 @@
         pltpu.make_async_copy(fitted.at[at, :], fitted_out.at[at, :], out_sem.at[step]).wait()
 
 
-def owner(valid, mu_of, nu_of, arrived, metric, row_of, fb, occ):
-    rows = valid.shape[0]
+def owner(number, arrived, metric, nbasis, columns, share, fb, occ):
+    rows = number.shape[0]
     owners = arrived.shape[0]
     capacity = rows // owners
-    nbasis = row_of.shape[0]
     ab = metric.shape[0]
     length = fb * ab * fb // 128
     rb = 32
@@ -284,15 +286,15 @@
     vmem = pl.BlockSpec(memory_space=pltpu.VMEM)
     anywhere = pl.BlockSpec(memory_space=pl.ANY)
     return pl.pallas_call(
-        functools.partial(owner_kernel, (rows, nbasis, fb, ab, occ, rb, capacity)),
+        functools.partial(owner_kernel, (rows, nbasis, fb, ab, occ, rb, capacity, columns, share)),
         out_shape=(
             jax.ShapeDtypeStruct((nbasis, wide), BF),
             jax.ShapeDtypeStruct((nbasis, nbasis), BF),
         ),
         grid_spec=pltpu.PrefetchScalarGridSpec(
-            num_scalar_prefetch=3,
+            num_scalar_prefetch=1,
             grid=(1,),
-            in_specs=[anywhere, vmem, vmem],
+            in_specs=[anywhere, vmem],
             out_specs=(anywhere, vmem),
             scratch_shapes=[
                 pltpu.VMEM((rows + 1, length, 128), BF),
@@ -313,7 +315,7 @@
         ),
         compiler_params=pltpu.CompilerParams(vmem_limit_bytes=60 << 20),
         name="owner",
-    )(valid, mu_of, nu_of, arrived, metric, row_of)
+    )(number, arrived, metric)
 
 
 def shards(three_center, panel, metric, screen, pair_blocks):
@@ -327,21 +329,22 @@
     capacity = 2
     targets = screen[:, :, 0]
     own_targets = lax.dynamic_index_in_dim(targets, own, 0, keepdims=False)
-    outgoing = pack(own_targets, three_center, panel.reshape(-1, 128), pair_count, capacity)
-    arrived = lax.all_to_all(outgoing, "pair", 0, 0, tiled=True)
-
     mine = targets == own
     before = jnp.cumsum(mine.astype(jnp.int32), axis=1) - mine.astype(jnp.int32)
     hits = mine[:, None, :] & (before[:, None, :] == jnp.arange(capacity)[None, :, None])
     flat = pair_count * capacity
-    valid = jnp.sum(hits.astype(jnp.int32), axis=2).reshape(flat)
-    mu_of = jnp.sum(jnp.where(hits, pair_blocks[:, None, :, 0], 0), axis=2).reshape(flat)
-    nu_of = jnp.sum(jnp.where(hits, pair_blocks[:, None, :, 1], 0), axis=2).reshape(flat)
+    blocks = nbasis // fb
+    number = pair_blocks[:, None, :, 0] * blocks + pair_blocks[:, None, :, 1] + 1
+    listed = jnp.sum(jnp.where(hits, number, 0), axis=2).reshape(flat)
 
     share = nbasis // (pair_count * column_count)
-    row_of = jnp.arange(nbasis).reshape(pair_count, column_count, share)
-    row_of = row_of.transpose(1, 0, 2).reshape(nbasis, 1)
-    fitted, partial = owner(valid, mu_of, nu_of, arrived, metric[0], row_of, fb, occ)
+    own_targets, listed = lax.optimization_barrier((own_targets, listed))
+    outgoing = pack(own_targets, three_center, panel.reshape(-1, 128), pair_count, capacity)
+    arrived = lax.all_to_all(outgoing, "pair", 0, 0, tiled=True)
+
+    fitted, partial = owner(
+        listed, arrived, metric[0], nbasis, column_count, share, fb, occ
+    )
     partial = lax.all_to_all(
         partial.reshape(column_count, nbasis // column_count, nbasis), "aux", 0, 0, tiled=True
     )

time: 284 us -> 277 us (0.975)
  blocking collectives: 34.7 us -> 233 us
  waiting for transfers between devices: 188 us -> 0 us
  starting transfers between devices: 11.4 us -> 0 us
  Pallas kernels: 41.6 us -> 36.6 us
    all_to_all x0 -> x1, blocking collectives: none -> 200 us  [shards(): arrived = lax.all_to_all(outgoing, 'pair', 0, 0, tiled=True)]
    all_to_all x1 -> x0, waiting for transfers between devices: 188 us -> none  [shards(): arrived = lax.all_to_all(outgoing, 'pair', 0, 0, tiled=True)]
    all_to_all x1 -> x0, starting transfers between devices: 11.4 us -> none  [shards(): arrived = lax.all_to_all(outgoing, 'pair', 0, 0, tiled=True)]
    pallas_call x1, Pallas kernels: 35.2 us -> 30.2 us  [owner(): pl.pallas_call(functools.partial(owner_kernel, (rows, nbasis, fb, ab, occ...]
  transfers between devices with their start and end apart: 1 -> 0, of which waited for: 1 -> 0; matrix products, arithmetic and copies ran while one was open for 1% -> 0% of each run, Pallas kernels for 0% -> 0%
where the time goes in v4:
time: 277 us; the launch traced here: 276 us
  blocking collectives  233 us (84%)
  Pallas kernels  36.6 us (13%)
  local copies, waits for them, and re-layouts  3.39 us (1%)
    all_to_all x1, blocking collectives, shards(): arrived = lax.all_to_all(outgoing, 'pair', 0, 0, tiled=True)  200 us
    pallas_call x1, Pallas kernels, owner(): pl.pallas_call(functools.partial(owner_kernel, (rows, nbasis, fb, ab, occ...  30.2 us
    all_to_all x1, blocking collectives, shards(): partial = lax.all_to_all(partial, 'pair', 0, 0, tiled=True)  17.8 us
    all_to_all x1, blocking collectives, shards(): lax.all_to_all(partial.reshape(column_count, nbasis // column_count, nbas...  15.3 us
    pallas_call x1, Pallas kernels, pack(): pl.pallas_call(functools.partial(pack_kernel, (slots, owners, capacity)),...  6.39 us

profile of v4, /device:TPU:32, one launch (start us, length us, event | category | flops | bytes accessed | tf_op | source)
XLA Modules:
  0.0 276.0 jit_solution(4816370786775054541)
XLA Ops:
  0.6 1.3 reshape.63.panel
  2.0 0.9 add_add_fusion
  2.8 1.2 dynamic-slice_bitcast_fusion.target
  4.0 0.7 fusion.1
  4.7 0.2 reduce_window_sum.11
  4.9 0.1 select_reduce_fusion
  5.1 0.1 copy.12
  5.1 0.7 reshape.62.number
  5.9 6.4 %pack.1 = bf16[32,1032,128]{2,1,0:T(8,128)(2,1)} custom-call(s32[32]{0:T(128)} %dynamic-slice_bitcast_fusion.target, bf16[32,32,2048]{2,1,0:T(8,128)(2,1)} %blocks.1, bf16[8,128]{1,0:T(8,128)(2,1)} %reshape.63.panel), custom_call_target="tpu_custom_call" | custom-call | tf_op jit(solution)/shard_map/pack/pallas_call | solution.py:82
  12.3 199.6 %all_to_all.15.arrived = bf16[32,1032,128]{2,1,0:T(8,128)(2,1)} all-to-all(bf16[32,1032,128]{2,1,0:T(8,128)(2,1)} %pack.1), channel_id=1, replica_groups=mesh['pair'=32,'aux'=8] {'pair'}, dimensions={0} | all-to-all | bytes 16908288 | tf_op jit(solution)/shard_map/all_to_all | solution.py:343
  211.9 30.2 %owner.1 = (bf16[512,4096]{1,0:T(8,128)(2,1)}, bf16[512,512]{1,0:T(8,128)(2,1)}) custom-call(s32[64]{0:T(128)} %reshape.62.number, bf16[32,1032,128]{2,1,0:T(8,128)(2,1)} %all_to_all.15.arrived, f32[64,64]{1,0:T(8,128)} %bitcast.12), custom_call_target="tpu_custom_call" | custom-call | tf_op jit(solution)/shard_map/owner/pallas_call | solution.py:288
  242.1 15.3 %all_to_all.16 = bf16[8,64,512]{2,1,0:T(8,128)(2,1)S(1)} all-to-all(bf16[8,64,512]{2,1,0:T(8,128)(2,1)} %bitcast.10), channel_id=1, replica_groups=mesh['pair'=32,'aux'=8] {'aux'}, dimensions={0} | all-to-all | bytes 1048576 | tf_op jit(solution)/shard_map/all_to_all | solution.py:348
  257.4 0.1 convert_reduce_fusion
  257.5 0.1 reshape.65
  257.6 17.8 %all_to_all.17 = f32[32,2,512]{2,1,0:T(2,128)S(1)} all-to-all(f32[32,2,512]{2,1,0:T(2,128)S(1)} %reshape.65), channel_id=1, replica_groups=mesh['pair'=32,'aux'=8] {'pair'}, dimensions={0} | all-to-all | bytes 262144 | tf_op jit(solution)/shard_map/all_to_all | solution.py:352
  275.3 0.1 reduce_sum.29
  275.4 0.6 broadcast_multiply_fusion
  (1 shorter events, 0.0 us)

commit v5 on v4

--- a/solution.py
+++ b/solution.py
@@ -9,7 +9,7 @@
 BF = jnp.bfloat16
 F32 = jnp.float32
 SUBS = 4
-GROUP = 4
+GROUP = 8
 WSTEP = 4
 YT = jnp.float32
 
@@ -30,7 +30,7 @@
     return jnp.dot(a, b, preferred_element_type=F32)
 
 
-def pack_kernel(sizes, target, blocks, panel, out, held, flat, seen, in_sem, out_sem, panel_sem):
+def pack_kernel(sizes, target, blocks, rows, out, held, flat, panel, seen, in_sem, out_sem, panel_sem):
     slots, owners, capacity = sizes
     fb = held.shape[1]
     tiles = held.shape[2] // 128
@@ -51,6 +51,10 @@
     @pl.loop(0, slots)
     def _(s):
         fetch(s).start()
+
+    lines = rows[...].astype(F32)
+    half = panel.shape[0]
+    panel[...] = jnp.concatenate([lines[:half], lines[half:]], axis=1).astype(panel.dtype)
 
     @pl.loop(0, owners)
     def _(p):
@@ -81,7 +85,7 @@
     length = fb * inner // 128
     return pl.pallas_call(
         functools.partial(pack_kernel, (slots, owners, capacity)),
-        out_shape=jax.ShapeDtypeStruct((owners, capacity * length + panel.shape[0], 128), blocks.dtype),
+        out_shape=jax.ShapeDtypeStruct((owners, capacity * length + panel.shape[0] // 2, 128), blocks.dtype),
         grid_spec=pltpu.PrefetchScalarGridSpec(
             num_scalar_prefetch=1,
             grid=(1,),
@@ -90,6 +94,7 @@
             scratch_shapes=[
                 pltpu.VMEM((slots, fb, inner), blocks.dtype),
                 pltpu.VMEM((slots, length, 128), blocks.dtype),
+                pltpu.VMEM((panel.shape[0] // 2, 128), blocks.dtype),
                 pltpu.SMEM((owners,), jnp.int32),
                 pltpu.SemaphoreType.DMA((slots,)),
                 pltpu.SemaphoreType.DMA((slots,)),
@@ -159,8 +164,10 @@
     def _(r):
         acc[pl.ds(pl.multiple_of(r * 8, 8), 8), :] = jnp.zeros((8, wide), F32)
 
-    pick_row = ones_where(iota((fb, fb // 2), 0) // 2 == iota((fb, fb // 2), 1))
-    same_half = iota((fb, 128), 0) % 2 == iota((fb, 128), 1) // occ
+    near = panel.shape[1]
+    row = iota((fb, fb // 2), 0)
+    pick_row = ones_where(row // (2 * near) * near + row % near == iota((fb, fb // 2), 1))
+    same_half = iota((fb, 128), 0) % (2 * near) // near == iota((fb, 128), 1) // occ
     spread_row = iota((128, 512), 0) % occ
     spread_col = iota((128, 512), 1)
     spread = ones_where((spread_col // 32) * 4 + spread_col % 4 == spread_row)
@@ -339,7 +346,7 @@
 
     share = nbasis // (pair_count * column_count)
     own_targets, listed = lax.optimization_barrier((own_targets, listed))
-    outgoing = pack(own_targets, three_center, panel.reshape(-1, 128), pair_count, capacity)
+    outgoing = pack(own_targets, three_center, panel, pair_count, capacity)
     arrived = lax.all_to_all(outgoing, "pair", 0, 0, tiled=True)
 
     fitted, partial = owner(

time: 277 us -> 274 us (0.989)
  no operation moved by 1% of the time
where the time goes in v5:
time: 274 us; the launch traced here: 273 us
  blocking collectives  231 us (84%)
  Pallas kernels  36.9 us (13%)
    all_to_all x1, blocking collectives, shards(): arrived = lax.all_to_all(outgoing, 'pair', 0, 0, tiled=True)  200 us
    pallas_call x1, Pallas kernels, owner(): pl.pallas_call(functools.partial(owner_kernel, (rows, nbasis, fb, ab, occ...  30.5 us
    all_to_all x1, blocking collectives, shards(): partial = lax.all_to_all(partial, 'pair', 0, 0, tiled=True)  16.9 us
    all_to_all x1, blocking collectives, shards(): lax.all_to_all(partial.reshape(column_count, nbasis // column_count, nbas...  14.7 us
    pallas_call x1, Pallas kernels, pack(): pl.pallas_call(functools.partial(pack_kernel, (slots, owners, capacity)),...  6.39 us

profile of v5, /device:TPU:32, one launch (start us, length us, event | category | flops | bytes accessed | tf_op | source)
XLA Modules:
  0.0 273.4 jit_solution(5234450009514732898)
XLA Ops:
  0.6 0.9 add_add_fusion
  1.5 1.2 dynamic-slice_bitcast_fusion.target
  2.7 0.7 fusion.1
  3.4 0.2 reduce_window_sum.11
  3.6 0.1 select_reduce_fusion
  3.7 0.1 copy.12
  3.8 0.6 reshape.59.number
  4.4 6.4 %pack.1 = bf16[32,1032,128]{2,1,0:T(8,128)(2,1)} custom-call(s32[32]{0:T(128)} %dynamic-slice_bitcast_fusion.target, bf16[32,32,2048]{2,1,0:T(8,128)(2,1)} %blocks.1, bf16[16,64]{1,0:T(8,128)(2,1)} %rows.1), custom_call_target="tpu_custom_call" | custom-call | tf_op jit(solution)/shard_map/pack/pallas_call | solution.py:86
  10.8 199.6 %all_to_all.15.arrived = bf16[32,1032,128]{2,1,0:T(8,128)(2,1)} all-to-all(bf16[32,1032,128]{2,1,0:T(8,128)(2,1)} %pack.1), channel_id=1, replica_groups=mesh['pair'=32,'aux'=8] {'pair'}, dimensions={0} | all-to-all | bytes 16908288 | tf_op jit(solution)/shard_map/all_to_all | solution.py:350
  210.4 30.5 %owner.1 = (bf16[512,4096]{1,0:T(8,128)(2,1)}, bf16[512,512]{1,0:T(8,128)(2,1)}) custom-call(s32[64]{0:T(128)} %reshape.59.number, bf16[32,1032,128]{2,1,0:T(8,128)(2,1)} %all_to_all.15.arrived, f32[64,64]{1,0:T(8,128)} %bitcast.12), custom_call_target="tpu_custom_call" | custom-call | tf_op jit(solution)/shard_map/owner/pallas_call | solution.py:295
  241.0 14.7 %all_to_all.16 = bf16[8,64,512]{2,1,0:T(8,128)(2,1)S(1)} all-to-all(bf16[8,64,512]{2,1,0:T(8,128)(2,1)} %bitcast.10), channel_id=1, replica_groups=mesh['pair'=32,'aux'=8] {'aux'}, dimensions={0} | all-to-all | bytes 1048576 | tf_op jit(solution)/shard_map/all_to_all | solution.py:355
  255.7 0.1 convert_reduce_fusion
  255.7 0.1 reshape.61
  255.8 16.9 %all_to_all.17 = f32[32,2,512]{2,1,0:T(2,128)S(1)} all-to-all(f32[32,2,512]{2,1,0:T(2,128)S(1)} %reshape.61), channel_id=1, replica_groups=mesh['pair'=32,'aux'=8] {'pair'}, dimensions={0} | all-to-all | bytes 262144 | tf_op jit(solution)/shard_map/all_to_all | solution.py:359
  272.7 0.1 reduce_sum.29
  272.8 0.6 broadcast_multiply_fusion
  (1 shorter events, 0.0 us)
